TPU v7x, 128 devices: a whole 4x4x4 slice. The times are simulated.
128 devices in a mesh: lon: 32 (over z, y, x_lo), lat: 4 (over x_hi, core).
Axes of the slice: x: 4 (x_hi: 2, x_lo: 2; x = x_hi * 2 + x_lo), y: 4, z: 4, core: 2. Of those that a mesh axis runs over, the one named last changes fastest.
Arguments:
- points: bfloat16 [256, 69, 5216], P('lat', None, 'lon'), may hold values from -6 to 6
- row_len: int32 [256], P('lat'), may hold values from 20 to 5136, as said below
- w_embed: bfloat16 [69, 256], replicated, may hold values from -0.75 to 0.75
- kernel1: bfloat16 [25, 256], replicated, may hold values from -1.1953125 to 1.1953125
- gain1: float32 [256], replicated, may hold values from 0.5 to 1.5
- point1: bfloat16 [256, 256], replicated, may hold values from -0.375 to 0.375
- kernel2: bfloat16 [25, 256], replicated, may hold values from -1.1953125 to 1.1953125
- gain2: float32 [256], replicated, may hold values from 0.5 to 1.5
- point2: bfloat16 [256, 256], replicated, may hold values from -0.375 to 0.375
- cotangent: bfloat16 [256, 768, 256], P('lat', 'lon'), may hold values from -6 to 6
Outputs:
- out: bfloat16 [256, 768, 256], P('lat', 'lon')
- grad_embed: float32 [69, 256], replicated
- grad_kernel1: float32 [25, 256], replicated
- grad_kernel2: float32 [25, 256], replicated
- grad_point1: float32 [256, 256], replicated
- grad_point2: float32 [256, 256], replicated
- grad_gain1: float32 [256], replicated
- grad_gain2: float32 [256], replicated
Inputs may be any that keep to these rules, and one draw needn't show every extreme that they name: `row_len`: every row holds 20 plus a multiple of 4 points; some row holds exactly 5136.
All inputs are finite; a program needn't handle non-finite values.
Results may differ from a plain program's by a relative error of at most 0.012.
Values may be sent and summed in bfloat16 or wider, within the bound.
No kernel may reach another device: no remote copies, remote signals or barrier semaphores. Data moves between devices by JAX's collectives and lax.ppermute only.
A program may use at most 128 MiB of HBM per device.

v0:
```python
import functools

import jax
import jax.numpy as jnp
from jax import lax
from jax.experimental import pallas as pl
from jax.experimental.pallas import tpu as pltpu
from jax.sharding import PartitionSpec as P

F32 = jnp.float32
BF16 = jnp.bfloat16
ROWS = 64
COLS = 24
HALO = 8
PITCH = COLS + 2 * HALO
TALL = ROWS + 2 * HALO
INNER = COLS + 8
LEAD = 16
FLAT = LEAD + PITCH * TALL + 16
SLIM = LEAD + INNER * TALL + 16
CHANS = 256
VARS = 69
TILES = 128
AXES = ("lon", "lat")


GROUP = 8 * COLS
STRIP = 8 * HALO


def regrid_kernel(
    row_len, sector, points, high, low, west, east, held, arrived, *, lon_total
):
    batch = held.shape[2]
    copies = [
        pltpu.make_async_copy(
            points.at[:, batch * i : batch * (i + 1)], held.at[i], arrived.at[i]
        )
        for i in range(held.shape[0])
    ]
    for copy in copies:
        copy.start()
    slots = points.shape[3]
    first = (sector[0] * COLS).astype(F32)
    whole = lon_total // 4
    lane = lax.broadcasted_iota(jnp.int32, (8, GROUP), 1)
    row = lane % 8
    cell = first + (lane // 8).astype(F32)
    own = lax.broadcasted_iota(jnp.int32, (8, GROUP), 0) == row
    mark = lax.broadcasted_iota(jnp.int32, (slots, GROUP), 0).astype(F32)
    for i, copy in enumerate(copies):
        found = []
        copy.wait()
        for k in range(batch):
            count = jnp.zeros((8, GROUP), F32)
            for q in range(8):
                length = row_len[8 * (batch * i + k) + q]
                count = jnp.where(row == q, length.astype(F32), count)
            product = cell * count
            lower = jnp.floor((product + 2.0) * (1.0 / lon_total))
            start = jnp.floor((first * count + 2.0) * (1.0 / lon_total))
            share = (product - lower * lon_total) * 0.25
            away = mark - (lower - start)[:1]
            mix = jnp.where(
                away == 0.0, whole - share[:1], jnp.where(away == 1.0, share[:1], 0.0)
            )
            rows = held[i, :, k].reshape(VARS * 8, slots)
            every = jnp.dot(rows, mix.astype(BF16), preferred_element_type=F32)
            kept = jnp.where(own[None], every.reshape(VARS, 8, GROUP), 0.0)
            found.append(jnp.sum(kept, 1) * (1.0 / whole))
        lanes = slice(batch * GROUP * i, batch * GROUP * (i + 1))
        edge = slice(batch * STRIP * i, batch * STRIP * (i + 1))
        values = jnp.concatenate(found, 1)
        rounded = values.astype(BF16)
        high[:, lanes] = rounded
        low[:, lanes] = (values - rounded.astype(F32)).astype(BF16)
        west[:, edge] = jnp.concatenate([f[:, :STRIP] for f in found], 1).astype(BF16)
        east[:, edge] = jnp.concatenate([f[:, GROUP - STRIP :] for f in found], 1).astype(BF16)


def regrid(points, row_len, lon_total):
    nvars, nrows, slots = points.shape
    batches = 4
    strips = jax.ShapeDtypeStruct((nvars, nrows * HALO), BF16)
    full = jax.ShapeDtypeStruct((nvars, nrows * COLS), BF16)
    smem = pl.BlockSpec(memory_space=pltpu.SMEM)
    vmem = pl.BlockSpec(memory_space=pltpu.VMEM)
    return pl.pallas_call(
        functools.partial(regrid_kernel, lon_total=lon_total),
        in_specs=[smem, smem, pl.BlockSpec(memory_space=pl.ANY)],
        out_specs=[vmem] * 4,
        out_shape=[full, full, strips, strips],
        scratch_shapes=[
            pltpu.VMEM((batches, nvars, nrows // (8 * batches), 8, slots), BF16),
            pltpu.SemaphoreType.DMA((batches,)),
        ],
        name="regrid",
    )(
        row_len,
        jnp.reshape(lax.axis_index("lon"), (1,)).astype(jnp.int32),
        points.reshape(nvars, nrows // 8, 8, slots),
    )


def at(row):
    return LEAD + PITCH * row


def inner(row):
    return LEAD + INNER * row


def conv(source, half, start, pitch, rows, cols, taps, visit=None):
    sums = [None] * rows
    for e in range(5):
        weights = [taps[half, 5 * a + e] for a in range(5)]
        for i in range(rows + 4):
            x = source[half, pl.ds(start + pitch * (i - 2) + e - 2, cols), :]
            x = x.reshape(cols // 8, 8, 128)
            for a in range(5):
                r = i - a
                if 0 <= r < rows:
                    term = x * weights[a]
                    sums[r] = term if sums[r] is None else sums[r] + term
                    if visit is not None:
                        visit(a, e, r, x)
        if visit is not None:
            visit(None, e, None, None)
    return sums


def own_tiles(x):
    later = lax.broadcasted_iota(jnp.int32, (8, 128), 0) >= 4
    return jnp.stack([jnp.where(later, x[0], x[3]), x[1], x[2]])


class TapSums:
    def __init__(self, store, half, centre):
        self.store, self.half, self.centre, self.live = store, half, centre, {}
        self.seen = self.own = None

    def __call__(self, a, e, r, x):
        if a is None:
            for tap, value in self.live.items():
                self.store[self.half, tap] += value
            self.live = {}
            return
        tap = 24 - (5 * a + e)
        if x.shape[0] == 4:
            if self.seen is not x:
                self.seen, self.own = x, own_tiles(x)
            x = self.own
        term = jnp.sum(self.centre[r] * x, 0)
        self.live[tap] = term if tap not in self.live else self.live[tap] + term


def blocks_kernel(
    lat, high, low, left, right, near, far, cot, cot_left, cot_right,
    w_embed, kernel1, gain1, point1, kernel2, gain2, point2,
    out, packed,
    x0, cots, d, h1, xhat1, scale1, slope1, dd2, g1, dd1,
    taps1, taps2, flip1, flip2, half1, half2, turned1, turned2,
    u1, dp1, u2, dp2, g0, gk1, gk2, gg1, gg2, swap, lifted,
    *, lat_devices,
):
    halves = (slice(0, 128), slice(128, 256))

    for k in range(25):
        for h in (0, 1):
            one = jnp.broadcast_to(kernel1[k : k + 1, halves[h]].astype(F32), (8, 128))
            two = jnp.broadcast_to(kernel2[k : k + 1, halves[h]].astype(F32), (8, 128))
            taps1[h, k] = one
            flip1[h, 24 - k] = one
            taps2[h, k] = two
            flip2[h, 24 - k] = two
    for point, half, turned in ((point1, half1, turned1), (point2, half2, turned2)):
        value = point[...].astype(F32) * 0.5
        half[...] = value.astype(BF16)
        turned[...] = jnp.transpose(value).astype(BF16)
    zeros = jnp.zeros((8, 128), F32)
    for h in (0, 1):
        for ref in (gg1, gg2):
            ref[h] = zeros
        for ref in (gk1, gk2):
            ref[h] = jnp.zeros((25, 8, 128), F32)
        for ref, size in ((x0, FLAT), (h1, FLAT), (dd2, SLIM), (dd1, SLIM)):
            ref[h, 0:LEAD] = jnp.zeros((LEAD, 128), F32)
            ref[h, size - 16 : size] = jnp.zeros((16, 128), F32)

    weight = w_embed[...]

    def across(a, b):
        return lax.dot_general(a, b, (((0,), (0,)), ((), ())), preferred_element_type=F32)

    def embed(spot, values):
        values = values.astype(BF16).astype(F32)
        for h in (0, 1):
            swap[h, pl.ds(pl.multiple_of(spot, 64), values.shape[0]), :] = values[:, halves[h]]

    def spread(spot, row):
        for k in range(8):
            for h in (0, 1):
                x0[h, pl.ds(pl.multiple_of(at(row + k), 8), PITCH), :] = swap[
                    h, pl.ds(spot + k, PITCH, stride=8), :
                ]

    for i in range(ROWS // 16):
        edge = slice(2 * STRIP * i, 2 * STRIP * (i + 1))
        middle = slice(2 * GROUP * i, 2 * GROUP * (i + 1))
        west = across(left[:, edge], weight)
        east = across(right[:, edge], weight)
        centre = across(high[:, middle], weight) + across(low[:, middle], weight)
        for k in (0, 1):
            spot = 8 * PITCH * (2 * i + k)
            embed(spot, west[STRIP * k : STRIP * (k + 1)])
            embed(spot + STRIP, centre[GROUP * k : GROUP * (k + 1)])
            embed(spot + STRIP + GROUP, east[STRIP * k : STRIP * (k + 1)])
    odd = lat[0] % 2 == 1

    def beyond(k, rows, lanes=slice(None)):
        one, two = near[rows, lanes].astype(F32), far[rows, lanes].astype(F32)
        return jnp.where(odd, two, one) if k else jnp.where(odd, one, two)

    for k in (0, 1):
        spot = 8 * PITCH * (ROWS // 8 + k)
        main = beyond(k, slice(128, 128 + VARS)).astype(BF16)
        rest = beyond(k, slice(208, 208 + VARS), slice(0, 8 * PITCH - CHANS)).astype(BF16)
        embed(spot, across(main, weight))
        embed(spot + CHANS, across(rest, weight))

    def unravel(i, carry):
        spread(8 * PITCH * i, HALO + 8 * i)
        return carry

    lax.fori_loop(0, ROWS // 8, unravel, 0)
    spread(8 * PITCH * (ROWS // 8), 0)
    spread(8 * PITCH * (ROWS // 8 + 1), HALO + ROWS)

    later = lax.broadcasted_iota(jnp.int32, (8, 128), 0) >= 4

    def put(row, value):
        for h in (0, 1):
            cots[h, pl.ds(pl.multiple_of(inner(row), 8), INNER), :] = value[:, halves[h]]

    def fill(pair, carry):
        sides = [cot_left[pair].astype(F32), cot_right[pair].astype(F32)]
        for odd in (0, 1):
            row = 2 * pair + odd
            edges = [s[4 * odd : 4 * odd + 4] for s in sides]
            put(
                row + HALO, jnp.concatenate([edges[0], cot[row].astype(F32), edges[1]], 0)
            )
        return carry

    lax.fori_loop(0, ROWS // 2, fill, 0)
    for k in range(4):
        rows = slice(INNER * k, INNER * (k + 1))
        put(k + 4, beyond(0, rows))
        put(k + HALO + ROWS, beyond(1, rows))

    def get(ref, start, count):
        return [ref[h, pl.ds(pl.multiple_of(start, 8), count), :] for h in (0, 1)]

    def keep(ref, start, values):
        for h in (0, 1):
            ref[h, pl.ds(pl.multiple_of(start, 8), values[h].shape[0]), :] = values[h]

    def from_wide(ref, row, rows):
        return [
            jnp.concatenate(
                [ref[h, pl.ds(at(row + r) + 4, INNER), :] for r in range(rows)], 0
            )
            for h in (0, 1)
        ]

    def joined(sums):
        return jnp.concatenate(sums, 0).reshape(-1, 128)

    def local_part(x):
        x = x.reshape(-1, 4, 8, 128)
        ends = jnp.where(later, x[:, 0], x[:, 3])
        return jnp.stack([ends, x[:, 1], x[:, 2]], 1).reshape(-1, 128)

    def gains(ref):
        return [ref[:, halves[h]] for h in (0, 1)]

    def normalised(raw):
        mean = jnp.sum(raw[0] * raw[0] + raw[1] * raw[1], -1, keepdims=True) * (1.0 / CHANS)
        scale = lax.rsqrt(mean + 1e-06)
        return scale, [raw[h] * scale for h in (0, 1)]

    def activated(xhat, gain, point):
        u = [xhat[h] * gain[h] for h in (0, 1)]
        p = jnp.dot(
            jnp.concatenate(u, 1).astype(BF16), point[...], preferred_element_type=F32
        )
        p = [p[:, s] for s in halves]
        rise = [jnp.tanh(v) + 1.0 for v in p]
        silu = [p[h] * rise[h] for h in (0, 1)]
        slope = [rise[h] + silu[h] * (2.0 - rise[h]) for h in (0, 1)]
        return u, silu, slope

    def through_norm(grad, slope, xhat, scale, gain, turned):
        dp = [grad[h] * slope[h] for h in (0, 1)]
        du = jnp.dot(
            jnp.concatenate(dp, 1).astype(BF16), turned[...], preferred_element_type=F32
        )
        gained = [du[:, halves[h]] * gain[h] for h in (0, 1)]
        both = [gained[h] * xhat[h] for h in (0, 1)]
        mean = jnp.sum(both[0] + both[1], -1, keepdims=True) * (1.0 / CHANS)
        dd = [
            (scale * (gained[h] - xhat[h] * mean)).astype(BF16).astype(F32) for h in (0, 1)
        ]
        return dp, both, dd

    def gain_sums(store, both):
        for h in (0, 1):
            store[h] += jnp.sum(local_part(both[h]).reshape(-1, 8, 128), 0)

    def pipeline(blocks, first, second):
        first(0)

        def step(i, carry):
            second(i - 1)
            first(i)
            return carry

        lax.fori_loop(1, blocks, step, 0)
        second(blocks - 1)

    size = 4 * PITCH

    def first_conv(i):
        start = at(2) + i * size
        keep(d, start, [joined(conv(x0, h, start, PITCH, 4, PITCH, taps1)) for h in (0, 1)])

    def first_mix(i):
        start = at(2) + i * size
        scale, xhat = normalised(get(d, start, size))
        _, silu, slope = activated(xhat, gains(gain1), half1)
        x = get(x0, start, size)
        keep(h1, start, [(x[h] + silu[h]).astype(BF16).astype(F32) for h in (0, 1)])
        keep(xhat1, start, xhat)
        keep(slope1, start, slope)
        scale1[pl.ds(pl.multiple_of(start, 8), size), :] = jnp.broadcast_to(scale, (size, 128))

    pipeline((TALL - 4) // 4, first_conv, first_mix)

    @pl.when(lat[0] == 0)
    def _():
        for h in (0, 1):
            h1[h, at(2) : at(HALO)] = jnp.zeros((6 * PITCH, 128), F32)

    @pl.when(lat[0] == lat_devices - 1)
    def _():
        for h in (0, 1):
            h1[h, at(HALO + ROWS) : at(HALO + ROWS + 6)] = jnp.zeros((6 * PITCH, 128), F32)

    def second_conv(row):
        keep(
            d,
            inner(row),
            [joined(conv(h1, h, at(row) + 4, PITCH, 4, INNER, taps2)) for h in (0, 1)],
        )

    def second_mix(row, local):
        start = inner(row)
        scale, xhat = normalised(get(d, start, 4 * INNER))
        gain = gains(gain2)
        u, silu, slope = activated(xhat, gain, half2)
        dp, both, dd = through_norm(
            get(cots, start, 4 * INNER), slope, xhat, scale, gain, turned2
        )
        keep(dd2, start, dd)
        if local is not None:
            keep(lifted, LEAD + 4 * INNER * local, silu)
            spot = pl.ds(pl.multiple_of(local * 96, 96), 96)
            u2[spot] = jnp.concatenate([local_part(v) for v in u], 1).astype(BF16)
            dp2[spot] = jnp.concatenate([local_part(v) for v in dp], 1).astype(BF16)
            gain_sums(gg2, both)

    def result(i):
        total = []
        for h in (0, 1):
            rows = []
            for r in range(4):
                place = LEAD + INNER * (4 * i + r) + 4
                base = h1[h, pl.ds(pl.multiple_of(at(HALO + 4 * i + r) + HALO, 8), COLS), :]
                rows.append(base + lifted[h, pl.ds(place, COLS), :])
            total.append(jnp.concatenate(rows, 0))
        out[pl.ds(i * 4, 4)] = jnp.concatenate(total, 1).reshape(4, COLS, CHANS).astype(BF16)

    for row in (4, HALO + ROWS):
        second_conv(row)
    for row in (4, HALO + ROWS):
        second_mix(row, None)
    pipeline(
        ROWS // 4,
        lambda i: second_conv(HALO + 4 * i),
        lambda i: second_mix(HALO + 4 * i, i),
    )

    def third_conv(row, rows, local):
        start = inner(row)
        total = []
        for h in (0, 1):
            visit = None
            if local:
                centre = [
                    own_tiles(h1[h, pl.ds(at(row + r) + 4, INNER), :].reshape(4, 8, 128))
                    for r in range(rows)
                ]
                visit = TapSums(gk2, h, centre)
            sums = joined(conv(dd2, h, start, INNER, rows, INNER, flip2, visit))
            total.append(sums + cots[h, pl.ds(pl.multiple_of(start, 8), rows * INNER), :])
        keep(g1, start, total)

    def third_mix(row, rows, local):
        start = inner(row)
        gain = gains(gain1)
        xhat = from_wide(xhat1, row, rows)
        scale = jnp.concatenate(
            [scale1[pl.ds(at(row + r) + 4, INNER), :] for r in range(rows)], 0
        )
        dp, both, dd = through_norm(
            get(g1, start, rows * INNER), from_wide(slope1, row, rows), xhat, scale, gain, turned1
        )
        keep(dd1, start, dd)
        if local is not None:
            spot = pl.ds(pl.multiple_of(local * 96, 96), 96)
            u = [local_part(xhat[h] * gain[h]) for h in (0, 1)]
            u1[spot] = jnp.concatenate(u, 1).astype(BF16)
            dp1[spot] = jnp.concatenate([local_part(v) for v in dp], 1).astype(BF16)
            gain_sums(gg1, both)
            result(local)

    for row in (6, HALO + ROWS):
        third_conv(row, 2, False)
    for row in (6, HALO + ROWS):
        third_mix(row, 2, None)
    pipeline(
        ROWS // 4,
        lambda i: third_conv(HALO + 4 * i, 4, True),
        lambda i: third_mix(HALO + 4 * i, 4, i),
    )

    @pl.when(lat[0] == 0)
    def _():
        for h in (0, 1):
            dd1[h, inner(6) : inner(HALO)] = jnp.zeros((2 * INNER, 128), F32)

    @pl.when(lat[0] == lat_devices - 1)
    def _():
        for h in (0, 1):
            dd1[h, inner(HALO + ROWS) : inner(HALO + ROWS + 2)] = jnp.zeros(
                (2 * INNER, 128), F32
            )

    def fourth(i, carry):
        row = HALO + 4 * i
        for h in (0, 1):
            centre = [
                x0[h, pl.ds(pl.multiple_of(at(row + r) + HALO, 8), COLS), :].reshape(3, 8, 128)
                for r in range(4)
            ]
            sums = conv(dd1, h, inner(row) + 4, INNER, 4, COLS, flip1, TapSums(gk1, h, centre))
            for r in range(4):
                base = g1[h, pl.ds(inner(row + r) + 4, COLS), :]
                place = GROUP * (i // 2) + 4 * (i % 2) + r
                g0[h, pl.ds(place, COLS, stride=8), :] = sums[r].reshape(COLS, 128) + base
        return carry

    lax.fori_loop(0, ROWS // 4, fourth, 0)

    def pack(place, value):
        rows = value.shape[0]
        value = value.astype(BF16)
        for h in (0, 1):
            packed[place : place + rows // 8, h] = value[:, halves[h]].reshape(rows // 8, 8, 128)

    pack(0, across(u1[...], dp1[...]) * 0.5)
    pack(32, across(u2[...], dp2[...]) * 0.5)
    field = jnp.concatenate([g0[h] for h in (0, 1)], 1).astype(BF16)
    embedded = jnp.dot(high[...], field, preferred_element_type=F32)

    def gain_row(ref, gain):
        total = [jnp.sum(ref[h], 0, keepdims=True) for h in (0, 1)]
        return jnp.concatenate(total, 1) / gain[...]

    pack(
        64,
        jnp.concatenate(
            [embedded, gain_row(gg1, gain1), gain_row(gg2, gain2), jnp.zeros((1, CHANS), F32)], 0
        ),
    )
    for place, ref in ((73, gk1), (77, gk2)):
        total = jnp.concatenate([jnp.sum(ref[h], 1) for h in (0, 1)], 1)
        pack(place, jnp.concatenate([total, jnp.zeros((7, CHANS), F32)], 0))
    packed[81:TILES] = jnp.zeros((TILES - 81, 2, 8, 128), BF16)


def blocks(fields, weights, lat_devices):
    wide = pltpu.VMEM((2, FLAT, 128), F32)
    slim = pltpu.VMEM((2, SLIM, 128), F32)
    taps = pltpu.VMEM((2, 25, 8, 128), F32)
    square = pltpu.VMEM((CHANS, CHANS), BF16)
    local = pltpu.VMEM((ROWS * COLS, CHANS), BF16)
    eight = pltpu.VMEM((2, 8, 128), F32)
    lat = jnp.reshape(lax.axis_index("lat"), (1,)).astype(jnp.int32)
    operands = (*fields, *weights)
    vmem = pl.BlockSpec(memory_space=pltpu.VMEM)
    return pl.pallas_call(
        functools.partial(blocks_kernel, lat_devices=lat_devices),
        in_specs=[pl.BlockSpec(memory_space=pltpu.SMEM)] + [vmem] * len(operands),
        out_specs=[vmem, vmem],
        out_shape=[
            jax.ShapeDtypeStruct((ROWS, COLS, CHANS), BF16),
            jax.ShapeDtypeStruct((TILES, 2, 8, 128), BF16),
        ],
        scratch_shapes=[wide, slim, wide, wide, wide, pltpu.VMEM((FLAT, 128), F32), wide]
        + [slim] * 3
        + [taps] * 4
        + [square] * 4
        + [local] * 4
        + [pltpu.VMEM((2, ROWS * COLS, 128), F32)]
        + [taps] * 2
        + [eight] * 2
        + [pltpu.VMEM((2, PITCH * TALL, 128), F32)]
        + [pltpu.VMEM((2, LEAD + INNER * ROWS + 16, 128), F32)],
        compiler_params=pltpu.CompilerParams(vmem_limit_bytes=60 * 1024 * 1024),
        name="both_blocks",
    )(lat, *operands)


def unpack_kernel(packed, embed, kernel1, kernel2, point1, point2, gain1, gain2, *, factor):
    for h in (0, 1):
        lanes = slice(128 * h, 128 * h + 128)
        point1[:, lanes] = packed[0:32, h].astype(F32).reshape(CHANS, 128) * factor
        point2[:, lanes] = packed[32:64, h].astype(F32).reshape(CHANS, 128) * factor
        mixed = packed[64:73, h].astype(F32).reshape(72, 128) * factor
        embed[:, lanes] = mixed[:VARS]
        gain1[:, lanes] = mixed[VARS : VARS + 1]
        gain2[:, lanes] = mixed[VARS + 1 : VARS + 2]
        kernel1[:, lanes] = (packed[73:77, h].astype(F32).reshape(32, 128) * factor)[:25]
        kernel2[:, lanes] = (packed[77:81, h].astype(F32).reshape(32, 128) * factor)[:25]


def summed(packed, factor):
    devices = lax.axis_size(AXES)
    parts = lax.all_to_all(packed, AXES, 0, 0, tiled=True)
    mine = jnp.sum(parts.reshape(devices, -1, 2, 8, 128).astype(F32), 0).astype(BF16)
    total = lax.all_to_all(jnp.tile(mine, (devices, 1, 1, 1)), AXES, 0, 0, tiled=True)
    shapes = [(VARS, CHANS), (25, CHANS), (25, CHANS), (CHANS, CHANS), (CHANS, CHANS)]
    results = pl.pallas_call(
        functools.partial(unpack_kernel, factor=factor),
        out_shape=[jax.ShapeDtypeStruct(s, F32) for s in shapes + [(1, CHANS)] * 2],
        name="unpack",
    )(total)
    return (*results[:5], results[5].reshape(CHANS), results[6].reshape(CHANS))


def shifted(before, after, axis, wrap):
    devices = lax.axis_size(axis)
    up = [(i, (i + 1) % devices) for i in range(devices if wrap else devices - 1)]
    down = [(j, i) for i, j in up]
    return lax.ppermute(after, axis, up), lax.ppermute(before, axis, down)


def on_device(points, row_len, w_embed, kernel1, gain1, point1, kernel2, gain2, point2, cotangent):
    lon_total = COLS * lax.axis_size("lon")
    rows_total = ROWS * lax.axis_size("lat")
    cot_left, cot_right = shifted(
        cotangent[:, :4].reshape(ROWS // 2, 8, CHANS),
        cotangent[:, COLS - 4 :].reshape(ROWS // 2, 8, CHANS),
        "lon",
        True,
    )
    high, low, west, east = regrid(jnp.swapaxes(points, 0, 1), row_len, lon_total)
    left, right = shifted(west, east, "lon", True)

    def band(rows, pairs, lanes, edge):
        sides = [c[pairs].reshape(4, 4, CHANS) for c in (cot_left, cot_right)]
        given = jnp.concatenate([sides[0], cotangent[rows], sides[1]], 1).reshape(-1, CHANS)
        field = jnp.concatenate([left[:, edge], high[:, lanes], right[:, edge]], 1)
        pieces = [field[:, :CHANS], field[:, CHANS:]]
        pieces = [
            jnp.pad(x, ((0, 80 - VARS), (0, CHANS - x.shape[1]))) for x in pieces
        ]
        return jnp.concatenate([given, *pieces], 0)

    first_band = band(slice(0, 4), slice(0, 2), slice(0, GROUP), slice(0, STRIP))
    last_band = band(
        slice(ROWS - 4, ROWS),
        slice(ROWS // 2 - 2, ROWS // 2),
        slice(GROUP * (ROWS // 8 - 1), GROUP * (ROWS // 8)),
        slice(STRIP * (ROWS // 8 - 1), STRIP * (ROWS // 8)),
    )
    odd = lax.axis_index("lat") % 2 == 1
    sent = (jnp.where(odd, first_band, last_band), jnp.where(odd, last_band, first_band))
    swaps = []
    for start in (0, 1):
        pairs = [(i, i + 1) for i in range(start, lax.axis_size("lat") - 1, 2)]
        swaps.append(lax.ppermute(sent[start], "lat", pairs + [(j, i) for i, j in pairs]))
    above, below = swaps
    fields = (high, low, left, right, above, below, cotangent, cot_left, cot_right)
    weights = (
        w_embed, kernel1, gain1.reshape(1, CHANS), point1,
        kernel2, gain2.reshape(1, CHANS), point2,
    )
    out, packed = blocks(fields, weights, lax.axis_size("lat"))
    return (out, *summed(packed, float(rows_total * lon_total) ** (-0.5)))


def solution(mesh):
    in_specs = (
        P("lat", None, "lon"),
        P("lat"),
        P(),
        P(),
        P(),
        P(),
        P(),
        P(),
        P(),
        P("lat", "lon", None),
    )
    out_specs = (P("lat", "lon", None), P(), P(), P(), P(), P(), P(), P())
    return jax.shard_map(
        on_device, mesh=mesh, in_specs=in_specs, out_specs=out_specs, check_vma=False
    )
```

profile of v0, /device:TPU:1, one launch (start us, length us, event | category | flops | bytes accessed | tf_op | source)
XLA Modules:
  0.0 119.3 jit_solution(2640580919829928404)
XLA Ops:
  0.6 1.1 fusion.11
  1.8 8.0 %collective-permute-start.3 = (bf16[32,8,256]{2,1,0:T(8,128)(2,1)S(1)}, bf16[32,8,256]{2,1,0:T(8,128)(2,1)S(1)}, u32[]{:S(2)}, u32[]{:S(2)}) collective-permute-start(bf16[32,8,256]{2,1,0:T(8,128)(2,1)S(1)} %reshape.72), channel_id=1, source_target_pairs={{4,0},{8,4},{12,8},{16,12},{20,16},{24,20},{28,24},{32,28},{36,32}... | collective-permute-start | bytes 393224 | tf_op jit(solution)/shard_map/ppermute | solution.py:566
  9.9 0.1 collective-permute-start.2
  10.0 4.8 %regrid.1 = (bf16[69,1536]{1,0:T(8,128)(2,1)}, bf16[69,1536]{1,0:T(8,128)(2,1)}, bf16[69,512]{1,0:T(8,128)(2,1)}, bf16[69,512]{1,0:T(8,128)(2,1)}) custom-call(s32[64]{0:T(128)} %row_len.1, s32[1]{0:T(128)} %bitcast.1.sector, bf16[69,8,8,163]{3,2,1,0:T(8,128)(2,1)} %bitcast.11), custom_call_target="tpu_custom_call" | custom-call | tf_op jit(solution)/shard_map/regrid/pallas_call | solution.py:88
  14.8 0.1 collective-permute-start
  14.8 5.7 %collective-permute-start.1 = (bf16[69,512]{1,0:T(8,128)(2,1)}, bf16[69,512]{1,0:T(8,128)(2,1)S(1)}, u32[]{:S(2)}, u32[]{:S(2)}) collective-permute-start(bf16[69,512]{1,0:T(8,128)(2,1)} %get-tuple-element.24), channel_id=1, source_target_pairs={{4,0},{8,4},{12,8},{16,12},{20,16},{24,20},{28,24},{32,28},{36,32}... | collective-permute-start | bytes 211976 | tf_op jit(solution)/shard_map/ppermute | solution.py:566
  20.6 0.8 fusion.10
  21.4 0.9 fusion.12
  22.3 0.2 collective-permute-done.left
  22.5 0.0 copy-start
  22.5 0.1 fusion.15
  22.5 0.0 collective-permute-done.1.right
  22.6 0.0 copy-start.1
  22.6 0.1 fusion.16
  22.6 0.1 fusion.8
  22.7 0.0 collective-permute-done.3.cot_right
  22.7 0.0 copy-start.2
  22.8 0.0 collective-permute-done.2.cot_left
  22.8 0.0 copy-start.3
  22.9 0.1 pad_maximum_fusion
  22.9 0.1 broadcast_select_fusion
  23.0 7.1 %collective-permute-start.5 = (bf16[288,256]{1,0:T(8,128)(2,1)S(1)}, bf16[288,256]{1,0:T(8,128)(2,1)S(1)}, u32[]{:S(2)}, u32[]{:S(2)}) collective-permute-start(bf16[288,256]{1,0:T(8,128)(2,1)S(1)} %get-tuple-element.38), channel_id=1, source_target_pairs={{1,2},{2,1},{5,6},{6,5},{9,10},{10,9},{13,14},{14,13},{17,18},{18,... | collective-permute-start | bytes 442376 | tf_op jit(solution)/shard_map/ppermute | solution.py:603
  30.1 0.1 collective-permute-start.4
  30.2 2.7 %collective-permute-done.5.far = bf16[288,256]{1,0:T(8,128)(2,1)S(1)} collective-permute-done((bf16[288,256]{1,0:T(8,128)(2,1)S(1)}, bf16[288,256]{1,0:T(8,128)(2,1)S(1)}, u32[]{:S(2)}, u32[]{:S(2)}) %collective-permute-start.5) | collective-permute-done | bytes 147488 | tf_op jit(solution)/shard_map/ppermute | solution.py:603
  32.9 0.0 copy-start.4
  32.9 0.0 collective-permute-done.4.near
  32.9 0.0 copy-start.5
  32.9 0.0 copy-done
  32.9 0.0 copy-done.1
  32.9 0.0 copy-done.2
  32.9 0.0 copy-done.3
  32.9 0.6 copy-done.4
  33.6 0.0 copy-done.5
  33.6 43.2 %both_blocks.1 = (bf16[64,24,256]{2,1,0:T(8,128)(2,1)}, bf16[128,2,8,128]{3,2,1,0:T(8,128)(2,1)}) custom-call(s32[1]{0:T(128)} %bitcast.lat, bf16[69,1536]{1,0:T(8,128)(2,1)} %get-tuple-element.21.high, bf16[69,1536]{1,0:T(8,128)(2,1)} %get-tuple-element.22.low, bf16[69,512]{1,0:T(8,128)(2,1)} %copy-done, bf16[69,512]{1,0:T(8,128)(2,1)} %copy-done.1, ...), custom_call_target="tpu_custom_call" | custom-call | tf_op jit(solution)/shard_map/both_blocks/pallas_call | solution.py:512
  76.9 22.4 %all_to_all.10 = bf16[128,2,8,128]{3,2,1,0:T(8,128)(2,1)S(1)} all-to-all(bf16[128,2,8,128]{3,2,1,0:T(8,128)(2,1)} %get-tuple-element.26), channel_id=1, replica_groups=mesh['lon'=32,'lat'=4] {'lon','lat'}, dimensions={0} | all-to-all | bytes 1048576 | tf_op jit(solution)/shard_map/all_to_all | solution.py:550
  99.3 0.1 reduce_sum.12
  99.4 0.1 tile.2
  99.5 17.9 %all_to_all.11.packed = bf16[128,2,8,128]{3,2,1,0:T(8,128)(2,1)} all-to-all(bf16[128,2,8,128]{3,2,1,0:T(8,128)(2,1)S(1)} %tile.2), channel_id=1, replica_groups=mesh['lon'=32,'lat'=4] {'lon','lat'}, dimensions={0} | all-to-all | bytes 1048576 | tf_op jit(solution)/shard_map/all_to_all | solution.py:552
  117.4 1.9 %unpack.1 = (f32[69,256]{1,0:T(8,128)}, f32[25,256]{1,0:T(8,128)}, f32[25,256]{1,0:T(8,128)}, f32[256,256]{1,0:T(8,128)}, f32[256,256]{1,0:T(8,128)}, /*index=5*/f32[1,256]{1,0:T(1,128)}, f32[1,256]{1,0:T(1,128)}) custom-call(bf16[128,2,8,128]{3,2,1,0:T(8,128)(2,1)} %all_to_all.11.packed), custom_call_target="tpu_custom_call" | custom-call | tf_op jit(solution)/shard_map/unpack/pallas_call | solution.py:554
  (8 shorter events, 0.1 us)
Async XLA Ops:
  1.8 20.9 %collective-permute-start.3 = (bf16[32,8,256]{2,1,0:T(8,128)(2,1)S(1)}, bf16[32,8,256]{2,1,0:T(8,128)(2,1)S(1)}, u32[]{:S(2)}, u32[]{:S(2)}) collective-permute-start(bf16[32,8,256]{2,1,0:T(8,128)(2,1)S(1)} %reshape.72), channel_id=1, source_target_pairs={{4,0},{8,4},{12,8},{16,12},{20,16},{24,20},{28,24},{32,28},{36,32}... | collective-permute-start | bytes 393224 | tf_op jit(solution)/shard_map/ppermute | solution.py:566
  9.9 12.9 %collective-permute-start.2 = (bf16[32,8,256]{2,1,0:T(8,128)(2,1)S(1)}, bf16[32,8,256]{2,1,0:T(8,128)(2,1)S(1)}, u32[]{:S(2)}, u32[]{:S(2)}) collective-permute-start(bf16[32,8,256]{2,1,0:T(8,128)(2,1)S(1)} %reshape.70), channel_id=1, source_target_pairs={{0,4},{4,8},{8,12},{12,16},{16,20},{20,24},{24,28},{28,32},{32,36}... | collective-permute-start | bytes 393224 | tf_op jit(solution)/shard_map/ppermute | solution.py:566
  14.8 7.7 %collective-permute-start = (bf16[69,512]{1,0:T(8,128)(2,1)}, bf16[69,512]{1,0:T(8,128)(2,1)S(1)}, u32[]{:S(2)}, u32[]{:S(2)}) collective-permute-start(bf16[69,512]{1,0:T(8,128)(2,1)} %get-tuple-element.23), channel_id=1, source_target_pairs={{0,4},{4,8},{8,12},{12,16},{16,20},{20,24},{24,28},{28,32},{32,36}... | collective-permute-start | bytes 211976 | tf_op jit(solution)/shard_map/ppermute | solution.py:566
  14.8 7.7 %collective-permute-start.1 = (bf16[69,512]{1,0:T(8,128)(2,1)}, bf16[69,512]{1,0:T(8,128)(2,1)S(1)}, u32[]{:S(2)}, u32[]{:S(2)}) collective-permute-start(bf16[69,512]{1,0:T(8,128)(2,1)} %get-tuple-element.24), channel_id=1, source_target_pairs={{4,0},{8,4},{12,8},{16,12},{20,16},{24,20},{28,24},{32,28},{36,32}... | collective-permute-start | bytes 211976 | tf_op jit(solution)/shard_map/ppermute | solution.py:566
  22.5 10.4 %copy-start = (bf16[69,512]{1,0:T(8,128)(2,1)}, bf16[69,512]{1,0:T(8,128)(2,1)S(1)}, u32[]{:S(2)}) copy-start(bf16[69,512]{1,0:T(8,128)(2,1)S(1)} %collective-permute-done.left) | copy-start | bytes 211972
  22.6 10.4 %copy-start.1 = (bf16[69,512]{1,0:T(8,128)(2,1)}, bf16[69,512]{1,0:T(8,128)(2,1)S(1)}, u32[]{:S(2)}) copy-start(bf16[69,512]{1,0:T(8,128)(2,1)S(1)} %collective-permute-done.1.right) | copy-start | bytes 211972
  22.7 10.2 %copy-start.2 = (bf16[32,8,256]{2,1,0:T(8,128)(2,1)}, bf16[32,8,256]{2,1,0:T(8,128)(2,1)S(1)}, u32[]{:S(2)}) copy-start(bf16[32,8,256]{2,1,0:T(8,128)(2,1)S(1)} %collective-permute-done.3.cot_right) | copy-start | bytes 393220
  22.8 10.1 %copy-start.3 = (bf16[32,8,256]{2,1,0:T(8,128)(2,1)}, bf16[32,8,256]{2,1,0:T(8,128)(2,1)S(1)}, u32[]{:S(2)}) copy-start(bf16[32,8,256]{2,1,0:T(8,128)(2,1)S(1)} %collective-permute-done.2.cot_left) | copy-start | bytes 393220
  23.0 9.9 %collective-permute-start.5 = (bf16[288,256]{1,0:T(8,128)(2,1)S(1)}, bf16[288,256]{1,0:T(8,128)(2,1)S(1)}, u32[]{:S(2)}, u32[]{:S(2)}) collective-permute-start(bf16[288,256]{1,0:T(8,128)(2,1)S(1)} %get-tuple-element.38), channel_id=1, source_target_pairs={{1,2},{2,1},{5,6},{6,5},{9,10},{10,9},{13,14},{14,13},{17,18},{18,... | collective-permute-start | bytes 442376 | tf_op jit(solution)/shard_map/ppermute | solution.py:603
  30.1 2.8 %collective-permute-start.4 = (bf16[288,256]{1,0:T(8,128)(2,1)S(1)}, bf16[288,256]{1,0:T(8,128)(2,1)S(1)}, u32[]{:S(2)}, u32[]{:S(2)}) collective-permute-start(bf16[288,256]{1,0:T(8,128)(2,1)S(1)} %get-tuple-element.39), channel_id=1, source_target_pairs={{0,1},{2,3},{1,0},{3,2},{4,5},{6,7},{5,4},{7,6},{8,9},{10,11},{9,8... | collective-permute-start | bytes 442376 | tf_op jit(solution)/shard_map/ppermute | solution.py:603
  32.9 0.7 copy-start.4
  32.9 0.7 copy-start.5
where the time goes:
time: 120 us; the launch traced here: 119 us
  Pallas kernels  49.9 us (42%)
  blocking collectives  40.4 us (34%)
  starting transfers between devices  21.1 us (18%)
  local copies, waits for them, and re-layouts  3.87 us (3%)
  waiting for transfers between devices  2.92 us (2%)
    pallas_call x1, Pallas kernels, blocks(): pl.pallas_call(functools.partial(blocks_kernel, lat_devices=lat_devices),...  43.2 us
    all_to_all x1, blocking collectives, summed(): parts = lax.all_to_all(packed, AXES, 0, 0, tiled=True)  22.4 us
    all_to_all x1, blocking collectives, summed(): lax.all_to_all(jnp.tile(mine, (devices, 1, 1, 1)), AXES, 0, 0, tiled=True)  17.9 us
    ppermute x4, starting transfers between devices, shifted(): return (lax.ppermute(after, axis, up), lax.ppermute(before, axis, down))  13.9 us
    ppermute x2, starting transfers between devices, on_device(): lax.ppermute(sent[start], 'lat', pairs + [(j, i) for i, j in pairs])  7.19 us
    pallas_call x1, Pallas kernels, regrid(): pl.pallas_call(functools.partial(regrid_kernel, lon_total=lon_total), in_...  4.8 us
    ppermute x2, waiting for transfers between devices, on_device(): lax.ppermute(sent[start], 'lat', pairs + [(j, i) for i, j in pairs])  2.72 us
  transfers between devices with their start and end apart: 6, of which 2 were waited for; matrix products, arithmetic and copies ran while one was open for 2% of the time, Pallas kernels for 4%

commit v1 on v0

--- a/solution.py
+++ b/solution.py
@@ -569,14 +569,23 @@
 def on_device(points, row_len, w_embed, kernel1, gain1, point1, kernel2, gain2, point2, cotangent):
     lon_total = COLS * lax.axis_size("lon")
     rows_total = ROWS * lax.axis_size("lat")
-    cot_left, cot_right = shifted(
+    devices = lax.axis_size("lon")
+    lon_odd = lax.axis_index("lon") % 2 == 1
+
+    def swapped_along_lon(first, last):
+        sent = (jnp.where(lon_odd, first, last), jnp.where(lon_odd, last, first))
+        got = []
+        for start in (0, 1):
+            pairs = [(i, (i + 1) % devices) for i in range(start, devices, 2)]
+            got.append(lax.ppermute(sent[start], "lon", pairs + [(j, i) for i, j in pairs]))
+        return jnp.where(lon_odd, got[0], got[1]), jnp.where(lon_odd, got[1], got[0])
+
+    cot_left, cot_right = swapped_along_lon(
         cotangent[:, :4].reshape(ROWS // 2, 8, CHANS),
         cotangent[:, COLS - 4 :].reshape(ROWS // 2, 8, CHANS),
-        "lon",
-        True,
     )
     high, low, west, east = regrid(jnp.swapaxes(points, 0, 1), row_len, lon_total)
-    left, right = shifted(west, east, "lon", True)
+    left, right = swapped_along_lon(west, east)
 
     def band(rows, pairs, lanes, edge):
         sides = [c[pairs].reshape(4, 4, CHANS) for c in (cot_left, cot_right)]

time: 120 us -> 117 us (0.975)
  starting transfers between devices: 21.1 us -> 16.4 us
  waiting for transfers between devices: 2.92 us -> 6.82 us
  blocking collectives: 40.4 us -> 37.1 us
  other arithmetic: 0.34 us -> 2.58 us
  local copies, waits for them, and re-layouts: 3.87 us -> 2.67 us
    ppermute x4, starting transfers between devices: 13.9 us -> 9.83 us  [swapped_along_lon(): lax.ppermute(sent[start], 'lon', pairs + [(j, i) for i, j in pairs])]
    ppermute x4, waiting for transfers between devices: 0.2 us -> 4.1 us  [swapped_along_lon(): lax.ppermute(sent[start], 'lon', pairs + [(j, i) for i, j in pairs])]
    all_to_all x1, blocking collectives: 22.4 us -> 19.2 us  [summed(): parts = lax.all_to_all(packed, AXES, 0, 0, tiled=True)]
    select_n x0 -> x4, other arithmetic: none -> 2.16 us  [the longest x2 2.12 us: swapped_along_lon(): sent = (jnp.where(lon_odd, first, last), jnp.where(lon_odd, last, first))]
  transfers between devices with their start and end apart: 6 -> 6, of which waited for: 2 -> 2; matrix products, arithmetic and copies ran while one was open for 2% -> 3% of each run, Pallas kernels for 4% -> 4%
where the time goes in v1:
time: 117 us; the launch traced here: 116 us
  Pallas kernels  49.9 us (43%)
  blocking collectives  37.1 us (32%)
  starting transfers between devices  16.4 us (14%)
  waiting for transfers between devices  6.82 us (6%)
  local copies, waits for them, and re-layouts  2.67 us (2%)
  other arithmetic  2.58 us (2%)
    pallas_call x1, Pallas kernels, blocks(): pl.pallas_call(functools.partial(blocks_kernel, lat_devices=lat_devices),...  43.2 us
    all_to_all x1, blocking collectives, summed(): parts = lax.all_to_all(packed, AXES, 0, 0, tiled=True)  19.2 us
    all_to_all x1, blocking collectives, summed(): lax.all_to_all(jnp.tile(mine, (devices, 1, 1, 1)), AXES, 0, 0, tiled=True)  17.9 us
    ppermute x4, starting transfers between devices, swapped_along_lon(): lax.ppermute(sent[start], 'lon', pairs + [(j, i) for i, j in pairs])  9.83 us
    ppermute x2, starting transfers between devices, on_device(): lax.ppermute(sent[start], 'lat', pairs + [(j, i) for i, j in pairs])  6.6 us
    pallas_call x1, Pallas kernels, regrid(): pl.pallas_call(functools.partial(regrid_kernel, lon_total=lon_total), in_...  4.8 us
    ppermute x4, waiting for transfers between devices, swapped_along_lon(): lax.ppermute(sent[start], 'lon', pairs + [(j, i) for i, j in pairs])  4.1 us
    ppermute x2, waiting for transfers between devices, on_device(): lax.ppermute(sent[start], 'lat', pairs + [(j, i) for i, j in pairs])  2.72 us
  transfers between devices with their start and end apart: 6, of which 2 were waited for; matrix products, arithmetic and copies ran while one was open for 3% of the time, Pallas kernels for 4%

profile of v1, /device:TPU:1, one launch (start us, length us, event | category | flops | bytes accessed | tf_op | source)
XLA Modules:
  0.0 116.4 jit_solution(15453161949228001100)
XLA Ops:
  0.6 1.2 %broadcast_select_fusion.3 = (bf16[64,4,256]{2,1,0:T(4,128)(2,1)S(1)}, bf16[64,4,256]{2,1,0:T(4,128)(2,1)S(1)}) fusion(pred[]{:T(512)S(6)} %eq.9, bf16[64,24,256]{2,1,0:T(8,128)(2,1)} %cot.1), kind=kLoop, calls=%fused_computation.8 | loop fusion | flops 131072 | bytes 524289 | tf_op jit(solution)/shard_map/jit(_where)/select_n | solution.py:576
  1.9 8.0 %collective-permute-start.3 = (bf16[32,8,256]{2,1,0:T(8,128)(2,1)S(1)}, bf16[32,8,256]{2,1,0:T(8,128)(2,1)S(1)}, u32[]{:S(2)}, u32[]{:S(2)}) collective-permute-start(bf16[32,8,256]{2,1,0:T(8,128)(2,1)S(1)} %select_n.84), channel_id=1, source_target_pairs={{4,8},{12,16},{20,24},{28,32},{36,40},{44,48},{52,56},{60,64},{68,... | collective-permute-start | bytes 393224 | tf_op jit(solution)/shard_map/ppermute | solution.py:580
  9.9 0.1 collective-permute-start.2
  10.0 4.8 %regrid.1 = (bf16[69,1536]{1,0:T(8,128)(2,1)}, bf16[69,1536]{1,0:T(8,128)(2,1)}, bf16[69,512]{1,0:T(8,128)(2,1)}, bf16[69,512]{1,0:T(8,128)(2,1)}) custom-call(s32[64]{0:T(128)} %row_len.1, s32[1]{0:T(128)} %bitcast.1.sector, bf16[69,8,8,163]{3,2,1,0:T(8,128)(2,1)} %bitcast.11), custom_call_target="tpu_custom_call" | custom-call | tf_op jit(solution)/shard_map/regrid/pallas_call | solution.py:88
  14.8 0.9 broadcast_select_fusion.8
  15.8 1.7 %collective-permute-start.1 = (bf16[69,512]{1,0:T(8,128)(2,1)S(1)}, bf16[69,512]{1,0:T(8,128)(2,1)S(1)}, u32[]{:S(2)}, u32[]{:S(2)}) collective-permute-start(bf16[69,512]{1,0:T(8,128)(2,1)S(1)} %get-tuple-element.46), channel_id=1, source_target_pairs={{4,8},{12,16},{20,24},{28,32},{36,40},{44,48},{52,56},{60,64},{68,... | collective-permute-start | bytes 211976 | tf_op jit(solution)/shard_map/ppermute | solution.py:580
  17.5 0.0 collective-permute-start
  17.5 0.8 fusion.10
  18.3 0.9 fusion.11
  19.2 4.1 %collective-permute-done.1 = bf16[69,512]{1,0:T(8,128)(2,1)S(1)} collective-permute-done((bf16[69,512]{1,0:T(8,128)(2,1)S(1)}, bf16[69,512]{1,0:T(8,128)(2,1)S(1)}, u32[]{:S(2)}, u32[]{:S(2)}) %collective-permute-start.1) | collective-permute-done | bytes 70688 | tf_op jit(solution)/shard_map/ppermute | solution.py:580
  23.3 0.0 collective-permute-done
  23.3 0.0 copy-start.2
  23.3 0.0 copy-start.3
  23.3 0.1 fusion.14
  23.4 0.1 fusion.8
  23.5 0.1 fusion.9
  23.6 0.0 collective-permute-done.3
  23.6 0.0 collective-permute-done.2
  23.6 0.0 copy-start
  23.7 0.0 copy-start.1
  23.8 0.1 broadcast_select_fusion
  23.9 6.5 %collective-permute-start.5 = (bf16[288,256]{1,0:T(8,128)(2,1)S(1)}, bf16[288,256]{1,0:T(8,128)(2,1)S(1)}, u32[]{:S(2)}, u32[]{:S(2)}) collective-permute-start(bf16[288,256]{1,0:T(8,128)(2,1)S(1)} %get-tuple-element.40), channel_id=1, source_target_pairs={{1,2},{2,1},{5,6},{6,5},{9,10},{10,9},{13,14},{14,13},{17,18},{18,... | collective-permute-start | bytes 442376 | tf_op jit(solution)/shard_map/ppermute | solution.py:612
  30.4 0.1 collective-permute-start.4
  30.5 2.7 %collective-permute-done.5.far = bf16[288,256]{1,0:T(8,128)(2,1)S(1)} collective-permute-done((bf16[288,256]{1,0:T(8,128)(2,1)S(1)}, bf16[288,256]{1,0:T(8,128)(2,1)S(1)}, u32[]{:S(2)}, u32[]{:S(2)}) %collective-permute-start.5) | collective-permute-done | bytes 147488 | tf_op jit(solution)/shard_map/ppermute | solution.py:612
  33.2 0.0 copy-start.4
  33.2 0.0 collective-permute-done.4.near
  33.2 0.0 copy-start.5
  33.2 0.0 copy-done.2
  33.2 0.0 copy-done.3
  33.2 0.0 copy-done
  33.2 0.0 copy-done.1
  33.2 0.6 copy-done.4
  33.9 0.1 copy-done.5
  33.9 43.2 %both_blocks.1 = (bf16[64,24,256]{2,1,0:T(8,128)(2,1)}, bf16[128,2,8,128]{3,2,1,0:T(8,128)(2,1)}) custom-call(s32[1]{0:T(128)} %bitcast.lat, bf16[69,1536]{1,0:T(8,128)(2,1)} %get-tuple-element.21.high, bf16[69,1536]{1,0:T(8,128)(2,1)} %get-tuple-element.22.low, bf16[69,512]{1,0:T(8,128)(2,1)} %copy-done.3, bf16[69,512]{1,0:T(8,128)(2,1)} %copy-done.2, ...), custom_call_target="tpu_custom_call" | custom-call | tf_op jit(solution)/shard_map/both_blocks/pallas_call | solution.py:512
  77.2 19.2 %all_to_all.10 = bf16[128,2,8,128]{3,2,1,0:T(8,128)(2,1)S(1)} all-to-all(bf16[128,2,8,128]{3,2,1,0:T(8,128)(2,1)} %get-tuple-element.26), channel_id=1, replica_groups=mesh['lon'=32,'lat'=4] {'lon','lat'}, dimensions={0} | all-to-all | bytes 1048576 | tf_op jit(solution)/shard_map/all_to_all | solution.py:550
  96.4 0.1 reduce_sum.12
  96.5 0.1 tile.2
  96.6 17.9 %all_to_all.11.packed = bf16[128,2,8,128]{3,2,1,0:T(8,128)(2,1)} all-to-all(bf16[128,2,8,128]{3,2,1,0:T(8,128)(2,1)S(1)} %tile.2), channel_id=1, replica_groups=mesh['lon'=32,'lat'=4] {'lon','lat'}, dimensions={0} | all-to-all | bytes 1048576 | tf_op jit(solution)/shard_map/all_to_all | solution.py:552
  114.5 1.9 %unpack.1 = (f32[69,256]{1,0:T(8,128)}, f32[25,256]{1,0:T(8,128)}, f32[25,256]{1,0:T(8,128)}, f32[256,256]{1,0:T(8,128)}, f32[256,256]{1,0:T(8,128)}, /*index=5*/f32[1,256]{1,0:T(1,128)}, f32[1,256]{1,0:T(1,128)}) custom-call(bf16[128,2,8,128]{3,2,1,0:T(8,128)(2,1)} %all_to_all.11.packed), custom_call_target="tpu_custom_call" | custom-call | tf_op jit(solution)/shard_map/unpack/pallas_call | solution.py:554
  (11 shorter events, 0.2 us)
Async XLA Ops:
  1.9 21.7 %collective-permute-start.3 = (bf16[32,8,256]{2,1,0:T(8,128)(2,1)S(1)}, bf16[32,8,256]{2,1,0:T(8,128)(2,1)S(1)}, u32[]{:S(2)}, u32[]{:S(2)}) collective-permute-start(bf16[32,8,256]{2,1,0:T(8,128)(2,1)S(1)} %select_n.84), channel_id=1, source_target_pairs={{4,8},{12,16},{20,24},{28,32},{36,40},{44,48},{52,56},{60,64},{68,... | collective-permute-start | bytes 393224 | tf_op jit(solution)/shard_map/ppermute | solution.py:580
  9.9 13.7 %collective-permute-start.2 = (bf16[32,8,256]{2,1,0:T(8,128)(2,1)S(1)}, bf16[32,8,256]{2,1,0:T(8,128)(2,1)S(1)}, u32[]{:S(2)}, u32[]{:S(2)}) collective-permute-start(bf16[32,8,256]{2,1,0:T(8,128)(2,1)S(1)} %select_n.82), channel_id=1, source_target_pairs={{0,4},{8,12},{16,20},{24,28},{32,36},{40,44},{48,52},{56,60},{64,6... | collective-permute-start | bytes 393224 | tf_op jit(solution)/shard_map/ppermute | solution.py:580
  15.8 7.5 %collective-permute-start.1 = (bf16[69,512]{1,0:T(8,128)(2,1)S(1)}, bf16[69,512]{1,0:T(8,128)(2,1)S(1)}, u32[]{:S(2)}, u32[]{:S(2)}) collective-permute-start(bf16[69,512]{1,0:T(8,128)(2,1)S(1)} %get-tuple-element.46), channel_id=1, source_target_pairs={{4,8},{12,16},{20,24},{28,32},{36,40},{44,48},{52,56},{60,64},{68,... | collective-permute-start | bytes 211976 | tf_op jit(solution)/shard_map/ppermute | solution.py:580
  17.5 5.8 %collective-permute-start = (bf16[69,512]{1,0:T(8,128)(2,1)S(1)}, bf16[69,512]{1,0:T(8,128)(2,1)S(1)}, u32[]{:S(2)}, u32[]{:S(2)}) collective-permute-start(bf16[69,512]{1,0:T(8,128)(2,1)S(1)} %get-tuple-element.47), channel_id=1, source_target_pairs={{0,4},{8,12},{16,20},{24,28},{32,36},{40,44},{48,52},{56,60},{64,6... | collective-permute-start | bytes 211976 | tf_op jit(solution)/shard_map/ppermute | solution.py:580
  23.3 9.9 %copy-start.2 = (bf16[69,512]{1,0:T(8,128)(2,1)}, bf16[69,512]{1,0:T(8,128)(2,1)S(1)}, u32[]{:S(2)}) copy-start(bf16[69,512]{1,0:T(8,128)(2,1)S(1)} %get-tuple-element.44.right) | copy-start | bytes 211972
  23.3 9.9 %copy-start.3 = (bf16[69,512]{1,0:T(8,128)(2,1)}, bf16[69,512]{1,0:T(8,128)(2,1)S(1)}, u32[]{:S(2)}) copy-start(bf16[69,512]{1,0:T(8,128)(2,1)S(1)} %get-tuple-element.45.left) | copy-start | bytes 211972
  23.6 9.6 %copy-start = (bf16[32,8,256]{2,1,0:T(8,128)(2,1)}, bf16[32,8,256]{2,1,0:T(8,128)(2,1)S(1)}, u32[]{:S(2)}) copy-start(bf16[32,8,256]{2,1,0:T(8,128)(2,1)S(1)} %get-tuple-element.38.cot_left) | copy-start | bytes 393220
  23.7 9.6 %copy-start.1 = (bf16[32,8,256]{2,1,0:T(8,128)(2,1)}, bf16[32,8,256]{2,1,0:T(8,128)(2,1)S(1)}, u32[]{:S(2)}) copy-start(bf16[32,8,256]{2,1,0:T(8,128)(2,1)S(1)} %get-tuple-element.39.cot_right) | copy-start | bytes 393220
  23.9 9.3 %collective-permute-start.5 = (bf16[288,256]{1,0:T(8,128)(2,1)S(1)}, bf16[288,256]{1,0:T(8,128)(2,1)S(1)}, u32[]{:S(2)}, u32[]{:S(2)}) collective-permute-start(bf16[288,256]{1,0:T(8,128)(2,1)S(1)} %get-tuple-element.40), channel_id=1, source_target_pairs={{1,2},{2,1},{5,6},{6,5},{9,10},{10,9},{13,14},{14,13},{17,18},{18,... | collective-permute-start | bytes 442376 | tf_op jit(solution)/shard_map/ppermute | solution.py:612
  30.4 2.8 %collective-permute-start.4 = (bf16[288,256]{1,0:T(8,128)(2,1)S(1)}, bf16[288,256]{1,0:T(8,128)(2,1)S(1)}, u32[]{:S(2)}, u32[]{:S(2)}) collective-permute-start(bf16[288,256]{1,0:T(8,128)(2,1)S(1)} %get-tuple-element.41), channel_id=1, source_target_pairs={{0,1},{2,3},{1,0},{3,2},{4,5},{6,7},{5,4},{7,6},{8,9},{10,11},{9,8... | collective-permute-start | bytes 442376 | tf_op jit(solution)/shard_map/ppermute | solution.py:612
  33.2 0.6 copy-start.4
  33.2 0.7 copy-start.5
